TPU v7x, 512 devices: a whole 4x8x8 slice. The times are simulated.
512 devices in a mesh: tm: 4 (over x), tile: 128 (over z, y, core).
Axes of the slice: x: 4, y: 8, z: 8, core: 2. Of those that a mesh axis runs over, the one named last changes fastest.
Arguments:
- frames: bfloat16 [4, 128, 8, 16, 384], P('tm', 'tile'), may hold values from -6 to 6
- norm_gain: float32 [384], replicated, may hold values from 0.1 to 1.9
- conv_weight: bfloat16 [3, 3, 3, 384, 384], replicated, may hold values from -0.0625 to 0.0625
- conv_bias: float32 [384], replicated, may hold values from -3 to 3
Outputs:
- decoded: bfloat16 [4, 128, 8, 16, 384], P('tm', 'tile')
All inputs are finite; a program needn't handle non-finite values.
Results may differ from a plain program's by a relative error of at most 0.0055.
Values may be sent and summed in bfloat16 or wider, within the bound.
A program may use at most 64 MiB of HBM per device.

v0:
```python
import jax
import jax.numpy as jnp
from jax import lax
from jax.sharding import PartitionSpec as P

GRID_W = 8


def shifted(value, axis, by):
    count = lax.axis_size(axis)
    pairs = [(i, i + by) for i in range(count) if 0 <= i + by < count]
    return lax.ppermute(value, axis, pairs)


def activate(tile_values, norm_gain):
    values = tile_values.astype(jnp.float32)
    scale = lax.rsqrt(jnp.mean(values * values, axis=-1, keepdims=True) + 1e-06)
    return jax.nn.silu(values * scale * norm_gain).astype(jnp.bfloat16)


def select_band(length, step):
    if step < 0:
        return slice(length - 1, length)
    if step > 0:
        return slice(0, 1)
    return slice(0, length)


def border_direct(stack, grid_w):
    tall = stack.shape[1]
    broad = stack.shape[2]
    place = lax.axis_index("tile")
    tile_row = place // grid_w
    tile_col = place % grid_w
    grid_h = lax.axis_size("tile") // grid_w
    found = {}
    for row_step in (-1, 0, 1):
        for col_step in (-1, 0, 1):
            if row_step == 0 and col_step == 0:
                found[row_step, col_step] = stack
                continue
            sent = stack[:, select_band(tall, row_step), select_band(broad, col_step), :]
            moved = shifted(sent, "tile", -(row_step * grid_w + col_step))
            inside = (
                (tile_row + row_step >= 0)
                & (tile_row + row_step < grid_h)
                & (tile_col + col_step >= 0)
                & (tile_col + col_step < grid_w)
            )
            found[row_step, col_step] = jnp.where(inside, moved, jnp.zeros_like(moved))
    bands = [
        jnp.concatenate([found[row_step, -1], found[row_step, 0], found[row_step, 1]], axis=2)
        for row_step in (-1, 0, 1)
    ]
    return jnp.concatenate(bands, axis=1)


def border(stack):
    return border_direct(stack, GRID_W)


def apply_taps(padded, weight_time, total):
    tall = padded.shape[0] - 2
    broad = padded.shape[1] - 2
    chans = padded.shape[2]
    for row_tap in range(3):
        window = jnp.concatenate(
            [
                padded[row_tap : row_tap + tall, col_tap : col_tap + broad, :]
                for col_tap in range(3)
            ],
            axis=-1,
        )
        kernel = weight_time[row_tap].reshape(3 * chans, chans)
        total = total + jnp.dot(
            window.reshape(tall * broad, 3 * chans), kernel, preferred_element_type=jnp.float32
        )
    return total


def body(frames, norm_gain, conv_weight, conv_bias):
    activation = activate(frames[0, 0], norm_gain)
    tall, broad, chans = activation.shape
    empty = jnp.zeros((tall * broad, chans), jnp.float32)
    back_one = shifted(activation, "tm", 1)
    back_two = shifted(activation, "tm", 2)
    padded = border(jnp.stack([back_two, back_one, activation]))
    total = empty
    for time_tap in range(3):
        total = apply_taps(padded[time_tap], conv_weight[time_tap], total)
    decoded = (total + conv_bias).astype(jnp.bfloat16)
    return decoded.reshape(1, 1, tall, broad, chans)


def solution(mesh):
    placed = (P("tm", "tile", None, None, None), P(), P(), P())
    return jax.shard_map(
        body,
        mesh=mesh,
        in_specs=placed,
        out_specs=P("tm", "tile", None, None, None),
        check_vma=False,
    )
```

profile of v0, /device:TPU:257, one launch (start us, length us, event | category | flops | bytes accessed | tf_op | source)
XLA Modules:
  0.0 71.5 jit_solution(9063652178505238907)
XLA Ops:
  0.0 1.0 %fusion.4 = f32[8,16]{1,0:T(8,128)S(1)} fusion(bf16[1,1,8,16,384]{4,3,2,1,0:T(8,128)(2,1)} %param.4), kind=kLoop, calls=%fused_computation.24 | loop fusion | flops 147328 | bytes 98816 | tf_op jit(solution)/shard_map/reduce_sum | solution.py:17
  1.0 1.7 %fusion.11 = bf16[8,16,384]{2,1,0:T(8,128)(2,1)} fusion(bf16[1,1,8,16,384]{4,3,2,1,0:T(8,128)(2,1)} %param.4, f32[384]{0:T(512)} %param.5, f32[8,16]{1,0:T(8,128)S(1)} %add_rsqrt_fusion), kind=kLoop, calls=%fused_computation.31 | loop fusion | flops 393216 | bytes 198656 | tf_op jit(solution)/shard_map/convert_element_type | solution.py:18
  2.7 0.0 copy-start.6
  2.7 0.0 copy-start.7
  2.7 3.9 %collective-permute-start.1 = (bf16[8,16,384]{2,1,0:T(8,128)(2,1)}, bf16[8,16,384]{2,1,0:T(8,128)(2,1)}, u32[]{:S(2)}, u32[]{:S(2)}) collective-permute-start(bf16[8,16,384]{2,1,0:T(8,128)(2,1)} %fusion.11), channel_id=1, source_target_pairs={{0,128},{128,256},{256,384},{1,129},{129,257},{257,385},{2,130},{1... | collective-permute-start | bytes 294920 | tf_op jit(solution)/shard_map/ppermute | solution.py:12
  6.5 4.4 %collective-permute-start = (bf16[8,16,384]{2,1,0:T(8,128)(2,1)}, bf16[8,16,384]{2,1,0:T(8,128)(2,1)}, u32[]{:S(2)}, u32[]{:S(2)}) collective-permute-start(bf16[8,16,384]{2,1,0:T(8,128)(2,1)} %fusion.11), channel_id=1, source_target_pairs={{0,256},{128,384},{1,257},{129,385},{2,258},{130,386},{3,259},{131... | collective-permute-start | bytes 294920 | tf_op jit(solution)/shard_map/ppermute | solution.py:12
  10.9 5.2 %fusion.20 = (bf16[1,1,3,384,384]{4,3,2,1,0:T(8,128)(2,1)}, bf16[1,1,3,384,384]{4,3,2,1,0:T(8,128)(2,1)S(1)}, bf16[1,1,3,384,384]{4,3,2,1,0:T(8,128)(2,1)S(1)}, ...) fusion(bf16[3,3,3,384,384]{4,3,2,1,0:T(8,128)(2,1)} %param.6), kind=kLoop, calls=%fused_computation.61 | loop fusion | bytes 15925248 | tf_op jit(solution)/shard_map/slice | solution.py:74
  16.1 0.0 copy-done.6
  16.1 0.0 copy-done.7
  16.1 0.8 %fusion.19 = bf16[1,8,16,384]{3,2,1,0:T(8,128)(2,1)} fusion(bf16[1,1,8,16,384]{4,3,2,1,0:T(8,128)(2,1)S(1)} %copy-done.6, f32[384]{0:T(512)S(1)} %copy-done.7, f32[8,16]{1,0:T(8,128)S(1)} %add_rsqrt_fusion), kind=kLoop, calls=%fused_computation.39 | loop fusion | flops 393216 | bytes 198656 | tf_op jit(solution)/shard_map/convert_element_type | solution.py:18
  16.9 0.0 copy-start.5
  16.9 0.0 collective-permute-done.1
  16.9 0.0 collective-permute-done
  16.9 0.9 %pad_maximum_fusion.17 = (bf16[3,1,1,384]{3,2,1,0:T(2,128)(2,1)S(1)}, bf16[3,1,1,384]{3,2,1,0:T(2,128)(2,1)S(1)}, bf16[3,1,1,384]{3,2,1,0:T(2,128)(2,1)S(1)}, bf16[3,1,1,384]{3,2,1,0:T(2,128)(2,1)S(1)}) fusion(bf16[1,8,16,384]{3,2,1,0:T(8,128)(2,1)} %fusion.19, bf16[1,8,16,384]{3,2,1,0:T(8,128)(2,1)} %bitcast.2, bf16[1,8,16,384]{3,2,1,0:T(8,128)(2,1)} %bitcast.1), kind=kLoop, calls=%fused_computation.59 | loop fusion | flops 27648 | bytes 304128 | tf_op jit(solution)/shard_map/slice | solution.py:42
  17.8 0.8 %pad_maximum_fusion.12 = (bf16[3,1,16,384]{3,2,1,0:T(8,128)(2,1)S(1)}, bf16[3,1,16,384]{3,2,1,0:T(8,128)(2,1)S(1)}) fusion(bf16[1,8,16,384]{3,2,1,0:T(8,128)(2,1)} %fusion.19, bf16[1,8,16,384]{3,2,1,0:T(8,128)(2,1)} %bitcast.2, bf16[1,8,16,384]{3,2,1,0:T(8,128)(2,1)} %bitcast.1), kind=kLoop, calls=%fused_computation.48 | loop fusion | flops 73728 | bytes 368640 | tf_op jit(solution)/shard_map/slice | solution.py:42
  18.6 7.7 %collective-permute-start.9 = (bf16[3,1,1,384]{3,2,1,0:T(2,128)(2,1)S(1)}, bf16[3,1,1,384]{3,2,1,0:T(2,128)(2,1)S(1)}, u32[]{:S(2)}, u32[]{:S(2)}) collective-permute-start(bf16[3,1,1,384]{3,2,1,0:T(2,128)(2,1)S(1)} %get-tuple-element.20), channel_id=1, source_target_pairs={{9,0},{10,1},{11,2},{12,3},{13,4},{14,5},{15,6},{16,7},{17,8},{18,... | collective-permute-start | bytes 6920 | tf_op jit(solution)/shard_map/ppermute | solution.py:12
  26.3 1.0 %pad_maximum_fusion.11 = (bf16[3,8,1,384]{3,2,1,0:T(2,128)(2,1)S(1)}, bf16[3,8,1,384]{3,2,1,0:T(2,128)(2,1)S(1)}) fusion(bf16[1,8,16,384]{3,2,1,0:T(8,128)(2,1)} %fusion.19, bf16[1,8,16,384]{3,2,1,0:T(8,128)(2,1)} %bitcast.2, bf16[1,8,16,384]{3,2,1,0:T(8,128)(2,1)} %bitcast.1), kind=kLoop, calls=%fused_computation.47 | loop fusion | flops 110592 | bytes 331776 | tf_op jit(solution)/shard_map/slice | solution.py:42
  27.3 1.9 %collective-permute-start.8 = (bf16[3,1,16,384]{3,2,1,0:T(8,128)(2,1)S(1)}, bf16[3,1,16,384]{3,2,1,0:T(8,128)(2,1)S(1)}, u32[]{:S(2)}, u32[]{:S(2)}) collective-permute-start(bf16[3,1,16,384]{3,2,1,0:T(8,128)(2,1)S(1)} %get-tuple-element.22), channel_id=1, source_target_pairs={{8,0},{9,1},{10,2},{11,3},{12,4},{13,5},{14,6},{15,7},{16,8},{17,9... | collective-permute-start | bytes 110600 | tf_op jit(solution)/shard_map/ppermute | solution.py:12
  29.2 4.9 %collective-permute-start.7 = (bf16[3,1,1,384]{3,2,1,0:T(2,128)(2,1)S(1)}, bf16[3,1,1,384]{3,2,1,0:T(2,128)(2,1)S(1)}, u32[]{:S(2)}, u32[]{:S(2)}) collective-permute-start(bf16[3,1,1,384]{3,2,1,0:T(2,128)(2,1)S(1)} %get-tuple-element.18), channel_id=1, source_target_pairs={{7,0},{8,1},{9,2},{10,3},{11,4},{12,5},{13,6},{14,7},{15,8},{16,9}... | collective-permute-start | bytes 6920 | tf_op jit(solution)/shard_map/ppermute | solution.py:12
  34.1 3.8 %collective-permute-start.6 = (bf16[3,8,1,384]{3,2,1,0:T(2,128)(2,1)S(1)}, bf16[3,8,1,384]{3,2,1,0:T(2,128)(2,1)S(1)}, u32[]{:S(2)}, u32[]{:S(2)}) collective-permute-start(bf16[3,8,1,384]{3,2,1,0:T(2,128)(2,1)S(1)} %get-tuple-element.24), channel_id=1, source_target_pairs={{1,0},{2,1},{3,2},{4,3},{5,4},{6,5},{7,6},{8,7},{9,8},{10,9},{11,1... | collective-permute-start | bytes 55304 | tf_op jit(solution)/shard_map/ppermute | solution.py:12
  37.9 2.2 %collective-permute-start.5 = (bf16[3,8,1,384]{3,2,1,0:T(2,128)(2,1)S(1)}, bf16[3,8,1,384]{3,2,1,0:T(2,128)(2,1)S(1)}, u32[]{:S(2)}, u32[]{:S(2)}) collective-permute-start(bf16[3,8,1,384]{3,2,1,0:T(2,128)(2,1)S(1)} %get-tuple-element.23), channel_id=1, source_target_pairs={{0,1},{1,2},{2,3},{3,4},{4,5},{5,6},{6,7},{7,8},{8,9},{9,10},{10,1... | collective-permute-start | bytes 55304 | tf_op jit(solution)/shard_map/ppermute | solution.py:12
  40.1 0.0 collective-permute-done.9
  40.1 3.0 %collective-permute-start.4 = (bf16[3,1,1,384]{3,2,1,0:T(2,128)(2,1)S(1)}, bf16[3,1,1,384]{3,2,1,0:T(2,128)(2,1)S(1)}, u32[]{:S(2)}, u32[]{:S(2)}) collective-permute-start(bf16[3,1,1,384]{3,2,1,0:T(2,128)(2,1)S(1)} %get-tuple-element.19), channel_id=1, source_target_pairs={{0,7},{1,8},{2,9},{3,10},{4,11},{5,12},{6,13},{7,14},{8,15},{9,16}... | collective-permute-start | bytes 6920 | tf_op jit(solution)/shard_map/ppermute | solution.py:12
  43.1 0.0 collective-permute-done.7
  43.1 8.1 %collective-permute-start.3 = (bf16[3,1,16,384]{3,2,1,0:T(8,128)(2,1)S(1)}, bf16[3,1,16,384]{3,2,1,0:T(8,128)(2,1)S(1)}, u32[]{:S(2)}, u32[]{:S(2)}) collective-permute-start(bf16[3,1,16,384]{3,2,1,0:T(8,128)(2,1)S(1)} %get-tuple-element.21), channel_id=1, source_target_pairs={{0,8},{1,9},{2,10},{3,11},{4,12},{5,13},{6,14},{7,15},{8,16},{9,17... | collective-permute-start | bytes 110600 | tf_op jit(solution)/shard_map/ppermute | solution.py:12
  51.3 0.0 collective-permute-done.4
  51.3 3.4 %collective-permute-start.2 = (bf16[3,1,1,384]{3,2,1,0:T(2,128)(2,1)S(1)}, bf16[3,1,1,384]{3,2,1,0:T(2,128)(2,1)S(1)}, u32[]{:S(2)}, u32[]{:S(2)}) collective-permute-start(bf16[3,1,1,384]{3,2,1,0:T(2,128)(2,1)S(1)} %get-tuple-element.17), channel_id=1, source_target_pairs={{0,9},{1,10},{2,11},{3,12},{4,13},{5,14},{6,15},{7,16},{8,17},{9,1... | collective-permute-start | bytes 6920 | tf_op jit(solution)/shard_map/ppermute | solution.py:12
  54.7 7.5 %collective-permute-done.2 = bf16[3,1,1,384]{3,2,1,0:T(2,128)(2,1)S(1)} collective-permute-done((bf16[3,1,1,384]{3,2,1,0:T(2,128)(2,1)S(1)}, bf16[3,1,1,384]{3,2,1,0:T(2,128)(2,1)S(1)}, u32[]{:S(2)}, u32[]{:S(2)}) %collective-permute-start.2) | collective-permute-done | bytes 2336 | tf_op jit(solution)/shard_map/ppermute | solution.py:12
  62.2 0.0 collective-permute-done.6
  62.3 0.0 collective-permute-done.5
  62.4 0.0 collective-permute-done.8
  62.4 0.0 collective-permute-done.3
  62.4 0.0 copy-done.5
  62.4 1.3 %maximum_maximum_fusion = bf16[3,10,18,384]{3,2,1,0:T(8,128)(2,1)S(1)} fusion(bf16[3,1,1,384]{3,2,1,0:T(2,128)(2,1)S(1)} %broadcast_select_fusion.4, bf16[3,1,16,384]{3,2,1,0:T(8,128)(2,1)S(1)} %broadcast_select_fusion.2, bf16[3,1,1,384]{3,2,1,0:T(2,128)(2,1)S(1)} %broadcast_select_fusion.5, bf16[3,8,1,384]{3,2,1,0:T(2,128)(2,1)S(1)} %broadcast_select_fusion, ...), kind=kLoop, calls=%fused_computation.10 | loop fusion | flops 4561920 | bytes 829440 | tf_op jit(solution)/shard_map/concatenate | solution.py:55
  63.7 0.1 slice_bitcast_fusion
  63.8 0.0 copy-start.4
  63.8 0.1 fusion.23
  63.9 0.1 pad_maximum_fusion
  63.9 1.0 %copy-done.4 = bf16[1,1,3,384,384]{4,3,2,1,0:T(8,128)(2,1)S(1)} copy-done((bf16[1,1,3,384,384]{4,3,2,1,0:T(8,128)(2,1)S(1)}, bf16[1,1,3,384,384]{4,3,2,1,0:T(8,128)(2,1)}, u32[]{:S(2)}) %copy-start.4) | copy-done | bytes 884760
  64.9 0.3 fusion.24
  65.3 0.0 copy-start.2
  65.3 0.2 fusion.21
  65.5 0.0 copy-start.1
  65.5 0.9 %copy-done.2 = bf16[1,1,3,384,384]{4,3,2,1,0:T(8,128)(2,1)S(1)} copy-done((bf16[1,1,3,384,384]{4,3,2,1,0:T(8,128)(2,1)S(1)}, bf16[1,1,3,384,384]{4,3,2,1,0:T(8,128)(2,1)}, u32[]{:S(2)}) %copy-start.2) | copy-done | bytes 884760
  66.4 0.3 convolution_add_fusion.7
  66.8 0.0 copy-start
  66.8 0.0 copy-done.1
  66.8 0.3 convolution_add_fusion.6
  67.2 0.8 %copy-done = bf16[1,1,3,384,384]{4,3,2,1,0:T(8,128)(2,1)S(1)} copy-done((bf16[1,1,3,384,384]{4,3,2,1,0:T(8,128)(2,1)S(1)}, bf16[1,1,3,384,384]{4,3,2,1,0:T(8,128)(2,1)}, u32[]{:S(2)}) %copy-start) | copy-done | bytes 884760
  68.0 0.3 convolution_add_fusion.5
  68.3 0.3 convolution_add_fusion.4
  68.7 0.3 convolution_add_fusion.3
  69.0 0.3 convolution_add_fusion.2
  69.4 0.0 copy-start.3
  69.4 0.0 copy-start.8
  69.4 0.3 convolution_add_fusion.1
  69.8 0.8 %copy-done.3 = bf16[1,1,3,384,384]{4,3,2,1,0:T(8,128)(2,1)S(1)} copy-done((bf16[1,1,3,384,384]{4,3,2,1,0:T(8,128)(2,1)S(1)}, bf16[1,1,3,384,384]{4,3,2,1,0:T(8,128)(2,1)}, u32[]{:S(2)}) %copy-start.3) | copy-done | bytes 884760
  70.6 0.0 copy-done.8
  70.6 1.0 %fusion.1 = bf16[128,384]{1,0:T(8,128)(2,1)} fusion(f32[128,384]{1,0:T(8,128)S(1)} %convolution_add_fusion.1, bf16[128,1152]{1,0:T(8,128)(2,1)S(1)} %bitcast.98, bf16[1152,384]{1,0:T(8,128)(2,1)S(1)} %bitcast.96, f32[384]{0:T(512)S(1)} %copy-done.8), kind=kOutput, calls=%fused_computation.9 | convolution fusion | flops 113393664 | bytes 1476096 | tf_op jit(solution)/shard_map/dot_general | solution.py:75
  (16 shorter events, 0.4 us)
Async XLA Ops:
  2.7 13.4 %copy-start.6 = (bf16[1,1,8,16,384]{4,3,2,1,0:T(8,128)(2,1)S(1)}, bf16[1,1,8,16,384]{4,3,2,1,0:T(8,128)(2,1)}, u32[]{:S(2)}) copy-start(bf16[1,1,8,16,384]{4,3,2,1,0:T(8,128)(2,1)} %param.4) | copy-start | bytes 294916
  2.7 13.4 %copy-start.7 = (f32[384]{0:T(512)S(1)}, f32[384]{0:T(512)}, u32[]{:S(2)}) copy-start(f32[384]{0:T(512)} %param.5) | copy-start | bytes 4612
  2.7 14.2 %collective-permute-start.1 = (bf16[8,16,384]{2,1,0:T(8,128)(2,1)}, bf16[8,16,384]{2,1,0:T(8,128)(2,1)}, u32[]{:S(2)}, u32[]{:S(2)}) collective-permute-start(bf16[8,16,384]{2,1,0:T(8,128)(2,1)} %fusion.11), channel_id=1, source_target_pairs={{0,128},{128,256},{256,384},{1,129},{129,257},{257,385},{2,130},{1... | collective-permute-start | bytes 294920 | tf_op jit(solution)/shard_map/ppermute | solution.py:12
  6.5 10.4 %collective-permute-start = (bf16[8,16,384]{2,1,0:T(8,128)(2,1)}, bf16[8,16,384]{2,1,0:T(8,128)(2,1)}, u32[]{:S(2)}, u32[]{:S(2)}) collective-permute-start(bf16[8,16,384]{2,1,0:T(8,128)(2,1)} %fusion.11), channel_id=1, source_target_pairs={{0,256},{128,384},{1,257},{129,385},{2,258},{130,386},{3,259},{131... | collective-permute-start | bytes 294920 | tf_op jit(solution)/shard_map/ppermute | solution.py:12
  16.9 45.5 %copy-start.5 = (bf16[1,8,16,384]{3,2,1,0:T(8,128)(2,1)S(1)}, bf16[1,8,16,384]{3,2,1,0:T(8,128)(2,1)}, u32[]{:S(2)}) copy-start(bf16[1,8,16,384]{3,2,1,0:T(8,128)(2,1)} %fusion.19) | copy-start | bytes 294916
  18.6 21.5 %collective-permute-start.9 = (bf16[3,1,1,384]{3,2,1,0:T(2,128)(2,1)S(1)}, bf16[3,1,1,384]{3,2,1,0:T(2,128)(2,1)S(1)}, u32[]{:S(2)}, u32[]{:S(2)}) collective-permute-start(bf16[3,1,1,384]{3,2,1,0:T(2,128)(2,1)S(1)} %get-tuple-element.20), channel_id=1, source_target_pairs={{9,0},{10,1},{11,2},{12,3},{13,4},{14,5},{15,6},{16,7},{17,8},{18,... | collective-permute-start | bytes 6920 | tf_op jit(solution)/shard_map/ppermute | solution.py:12
  27.3 35.1 %collective-permute-start.8 = (bf16[3,1,16,384]{3,2,1,0:T(8,128)(2,1)S(1)}, bf16[3,1,16,384]{3,2,1,0:T(8,128)(2,1)S(1)}, u32[]{:S(2)}, u32[]{:S(2)}) collective-permute-start(bf16[3,1,16,384]{3,2,1,0:T(8,128)(2,1)S(1)} %get-tuple-element.22), channel_id=1, source_target_pairs={{8,0},{9,1},{10,2},{11,3},{12,4},{13,5},{14,6},{15,7},{16,8},{17,9... | collective-permute-start | bytes 110600 | tf_op jit(solution)/shard_map/ppermute | solution.py:12
  29.2 13.9 %collective-permute-start.7 = (bf16[3,1,1,384]{3,2,1,0:T(2,128)(2,1)S(1)}, bf16[3,1,1,384]{3,2,1,0:T(2,128)(2,1)S(1)}, u32[]{:S(2)}, u32[]{:S(2)}) collective-permute-start(bf16[3,1,1,384]{3,2,1,0:T(2,128)(2,1)S(1)} %get-tuple-element.18), channel_id=1, source_target_pairs={{7,0},{8,1},{9,2},{10,3},{11,4},{12,5},{13,6},{14,7},{15,8},{16,9}... | collective-permute-start | bytes 6920 | tf_op jit(solution)/shard_map/ppermute | solution.py:12
  34.1 28.1 %collective-permute-start.6 = (bf16[3,8,1,384]{3,2,1,0:T(2,128)(2,1)S(1)}, bf16[3,8,1,384]{3,2,1,0:T(2,128)(2,1)S(1)}, u32[]{:S(2)}, u32[]{:S(2)}) collective-permute-start(bf16[3,8,1,384]{3,2,1,0:T(2,128)(2,1)S(1)} %get-tuple-element.24), channel_id=1, source_target_pairs={{1,0},{2,1},{3,2},{4,3},{5,4},{6,5},{7,6},{8,7},{9,8},{10,9},{11,1... | collective-permute-start | bytes 55304 | tf_op jit(solution)/shard_map/ppermute | solution.py:12
  37.9 24.4 %collective-permute-start.5 = (bf16[3,8,1,384]{3,2,1,0:T(2,128)(2,1)S(1)}, bf16[3,8,1,384]{3,2,1,0:T(2,128)(2,1)S(1)}, u32[]{:S(2)}, u32[]{:S(2)}) collective-permute-start(bf16[3,8,1,384]{3,2,1,0:T(2,128)(2,1)S(1)} %get-tuple-element.23), channel_id=1, source_target_pairs={{0,1},{1,2},{2,3},{3,4},{4,5},{5,6},{6,7},{7,8},{8,9},{9,10},{10,1... | collective-permute-start | bytes 55304 | tf_op jit(solution)/shard_map/ppermute | solution.py:12
  40.1 11.2 %collective-permute-start.4 = (bf16[3,1,1,384]{3,2,1,0:T(2,128)(2,1)S(1)}, bf16[3,1,1,384]{3,2,1,0:T(2,128)(2,1)S(1)}, u32[]{:S(2)}, u32[]{:S(2)}) collective-permute-start(bf16[3,1,1,384]{3,2,1,0:T(2,128)(2,1)S(1)} %get-tuple-element.19), channel_id=1, source_target_pairs={{0,7},{1,8},{2,9},{3,10},{4,11},{5,12},{6,13},{7,14},{8,15},{9,16}... | collective-permute-start | bytes 6920 | tf_op jit(solution)/shard_map/ppermute | solution.py:12
  43.1 19.3 %collective-permute-start.3 = (bf16[3,1,16,384]{3,2,1,0:T(8,128)(2,1)S(1)}, bf16[3,1,16,384]{3,2,1,0:T(8,128)(2,1)S(1)}, u32[]{:S(2)}, u32[]{:S(2)}) collective-permute-start(bf16[3,1,16,384]{3,2,1,0:T(8,128)(2,1)S(1)} %get-tuple-element.21), channel_id=1, source_target_pairs={{0,8},{1,9},{2,10},{3,11},{4,12},{5,13},{6,14},{7,15},{8,16},{9,17... | collective-permute-start | bytes 110600 | tf_op jit(solution)/shard_map/ppermute | solution.py:12
  51.3 10.9 %collective-permute-start.2 = (bf16[3,1,1,384]{3,2,1,0:T(2,128)(2,1)S(1)}, bf16[3,1,1,384]{3,2,1,0:T(2,128)(2,1)S(1)}, u32[]{:S(2)}, u32[]{:S(2)}) collective-permute-start(bf16[3,1,1,384]{3,2,1,0:T(2,128)(2,1)S(1)} %get-tuple-element.17), channel_id=1, source_target_pairs={{0,9},{1,10},{2,11},{3,12},{4,13},{5,14},{6,15},{7,16},{8,17},{9,1... | collective-permute-start | bytes 6920 | tf_op jit(solution)/shard_map/ppermute | solution.py:12
  63.8 1.2 %copy-start.4 = (bf16[1,1,3,384,384]{4,3,2,1,0:T(8,128)(2,1)S(1)}, bf16[1,1,3,384,384]{4,3,2,1,0:T(8,128)(2,1)}, u32[]{:S(2)}) copy-start(bf16[1,1,3,384,384]{4,3,2,1,0:T(8,128)(2,1)} %get-tuple-element.12) | copy-start | bytes 2654212
  65.3 1.2 %copy-start.2 = (bf16[1,1,3,384,384]{4,3,2,1,0:T(8,128)(2,1)S(1)}, bf16[1,1,3,384,384]{4,3,2,1,0:T(8,128)(2,1)}, u32[]{:S(2)}) copy-start(bf16[1,1,3,384,384]{4,3,2,1,0:T(8,128)(2,1)} %get-tuple-element.11) | copy-start | bytes 2654212
  65.5 1.3 %copy-start.1 = (bf16[1,1,3,384,384]{4,3,2,1,0:T(8,128)(2,1)S(1)}, bf16[1,1,3,384,384]{4,3,2,1,0:T(8,128)(2,1)}, u32[]{:S(2)}) copy-start(bf16[1,1,3,384,384]{4,3,2,1,0:T(8,128)(2,1)} %get-tuple-element.10) | copy-start | bytes 2654212
  66.8 1.2 %copy-start = (bf16[1,1,3,384,384]{4,3,2,1,0:T(8,128)(2,1)S(1)}, bf16[1,1,3,384,384]{4,3,2,1,0:T(8,128)(2,1)}, u32[]{:S(2)}) copy-start(bf16[1,1,3,384,384]{4,3,2,1,0:T(8,128)(2,1)} %get-tuple-element.9) | copy-start | bytes 2654212
  69.4 1.2 %copy-start.3 = (bf16[1,1,3,384,384]{4,3,2,1,0:T(8,128)(2,1)S(1)}, bf16[1,1,3,384,384]{4,3,2,1,0:T(8,128)(2,1)}, u32[]{:S(2)}) copy-start(bf16[1,1,3,384,384]{4,3,2,1,0:T(8,128)(2,1)} %get-tuple-element.5) | copy-start | bytes 2654212
  69.4 1.2 %copy-start.8 = (f32[384]{0:T(512)S(1)}, f32[384]{0:T(512)}, u32[]{:S(2)}) copy-start(f32[384]{0:T(512)} %param.7) | copy-start | bytes 4612
where the time goes:
time: 72.3 us; the launch traced here: 71.5 us
  starting transfers between devices  43.2 us (60%)
  local copies, waits for them, and re-layouts  9.09 us (13%)
  other arithmetic  7.79 us (11%)
  waiting for transfers between devices  7.49 us (10%)
  matrix products  3.48 us (5%)
    ppermute x10, starting transfers between devices, shifted(): return lax.ppermute(value, axis, pairs)  43.2 us
    ppermute x10, waiting for transfers between devices, shifted(): return lax.ppermute(value, axis, pairs)  7.49 us
    slice x1, local copies, waits for them, and re-layouts, apply_taps(): kernel = weight_time[row_tap].reshape(3 * chans, chans)  5.2 us
    unnamed x18, local copies, waits for them, and re-layouts  3.54 us
    dot_general x9, matrix products, apply_taps(): jnp.dot(window.reshape(tall * broad, 3 * chans), kernel, preferred_elemen...  3.48 us
    slice x3, other arithmetic, border_direct(): stack[:, select_band(tall, row_step), select_band(broad, col_step), :]  2.67 us
    convert_element_type x2, other arithmetic, activate(): return jax.nn.silu(values * scale * norm_gain).astype(jnp.bfloat16)  2.43 us
  transfers between devices with their start and end apart: 10, of which 1 were waited for; matrix products, arithmetic and copies ran while one was open for 10% of the time, Pallas kernels for 0%

commit v1 on v0

v1 whole, which is shorter than its diff:
```python
import functools

import jax
import jax.numpy as jnp
from jax import lax
from jax.experimental import pallas as pl
from jax.experimental.pallas import tpu as pltpu
from jax.sharding import PartitionSpec as P

GRID_W = 8
LANES = 128
MESH = pl.DeviceIdType.MESH
F32 = jnp.float32
BF16 = jnp.bfloat16


def block_kernel(
    tall,
    broad,
    chans,
    frame_count,
    tile_count,
    frames_hbm,
    gain_hbm,
    weight_hbm,
    bias_hbm,
    out_ref,
    raw,
    gain,
    bias,
    weight,
    tile,
    act32,
    col_out,
    col_in,
    row_in,
    corner_out,
    corner_in,
    window,
    edge_window,
    acc,
    load_sem,
    weight_sem,
    edge_send,
    edge_recv,
    mid_send,
    mid_recv,
    col_send,
    col_recv,
    row_send,
    row_recv,
    corner_send,
    corner_recv,
):
    t = lax.axis_index("tm")
    i = lax.axis_index("tile")
    row = lax.div(i, GRID_W)
    col = lax.rem(i, GRID_W)
    grid_h = tile_count // GRID_W
    pixels = tall * broad
    last = pixels - broad

    def inside(dt, dr, dc):
        ok = None
        tests = []
        if dt > 0:
            tests.append(t + dt < frame_count)
        if dt < 0:
            tests.append(t + dt >= 0)
        if dr > 0:
            tests.append(row + dr < grid_h)
        if dr < 0:
            tests.append(row + dr >= 0)
        if dc > 0:
            tests.append(col + dc < GRID_W)
        if dc < 0:
            tests.append(col + dc >= 0)
        for test in tests:
            ok = test if ok is None else jnp.logical_and(ok, test)
        return ok

    def device(dt, dr, dc):
        return {"tm": t + dt, "tile": i + dr * GRID_W + dc}

    partners = [(dt, 0, 0) for dt in (-2, -1, 1, 2)]
    partners += [(dt, 0, dc) for dt in (-2, -1, 0, 1, 2) for dc in (-1, 1)]
    partners += [(0, dr, dc) for dr in (-1, 1) for dc in (-1, 0, 1)]

    barrier = pltpu.get_barrier_semaphore()
    count = jnp.int32(0)
    for offset in partners:
        ok = inside(*offset)
        count = count + ok.astype(jnp.int32)

        @pl.when(ok)
        def _(offset=offset):
            pl.semaphore_signal(barrier, 1, device_id=device(*offset), device_id_type=MESH)

    loads = [
        pltpu.make_async_copy(frames_hbm, raw, load_sem.at[0]),
        pltpu.make_async_copy(gain_hbm, gain, load_sem.at[1]),
        pltpu.make_async_copy(bias_hbm, bias, load_sem.at[2]),
    ]
    for load in loads:
        load.start()
    weight_loads = [
        pltpu.make_async_copy(
            weight_hbm.at[pl.ds(6 - 3 * s, 3)], weight.at[pl.ds(6 - 3 * s, 3)], weight_sem.at[s]
        )
        for s in range(3)
    ]
    for load in weight_loads:
        load.start()
    for load in loads:
        load.wait()

    def activate(start, size):
        values = raw[start : start + size, :].astype(F32)
        scale = lax.rsqrt(jnp.mean(values * values, axis=-1, keepdims=True) + 1e-06)
        result = jax.nn.silu(values * scale * gain[...].reshape(1, chans)).astype(BF16)
        tile[0, start : start + size, :] = result
        for j in range(chans // LANES):
            act32[j, start : start + size, :] = result[:, j * LANES : (j + 1) * LANES].astype(F32)

    activate(0, pixels)
    for side in (0, 1):
        for j in range(chans // LANES):
            column = act32[j, pl.ds(side * (broad - 1), tall, stride=broad), :]
            col_out[side, :, j * LANES : (j + 1) * LANES] = column.astype(BF16)

    pl.semaphore_wait(barrier, count)

    def remote(src, dst, send, recv, offset):
        return pltpu.make_async_remote_copy(
            src_ref=src,
            dst_ref=dst,
            send_sem=send,
            recv_sem=recv,
            device_id=device(*offset),
            device_id_type=MESH,
        )

    edges = (pl.ds(0, broad), pl.ds(last, broad))
    middle = pl.ds(broad, pixels - 2 * broad)

    def edge_copy(s, k):
        return remote(
            tile.at[0, edges[k]], tile.at[s, edges[k]], edge_send.at[s, k], edge_recv.at[s, k], (s, 0, 0)
        )

    def mid_copy(s):
        return remote(tile.at[0, middle], tile.at[s, middle], mid_send.at[s], mid_recv.at[s], (s, 0, 0))

    def col_copy(s, side):
        return remote(
            col_out.at[side],
            col_in.at[s, 1 - side],
            col_send.at[s, side],
            col_recv.at[s, 1 - side],
            (s, 0, 2 * side - 1),
        )

    def row_copy(s, side):
        return remote(
            tile.at[s, edges[side]],
            row_in.at[s, 1 - side],
            row_send.at[s, side],
            row_recv.at[s, 1 - side],
            (0, 2 * side - 1, 0),
        )

    def corner_copy(s, side, end):
        return remote(
            corner_out.at[s, 2 * side + end],
            corner_in.at[s, 3 - 2 * side - end],
            corner_send.at[s, 2 * side + end],
            corner_recv.at[s, 3 - 2 * side - end],
            (0, 2 * side - 1, 2 * end - 1),
        )

    def guard(ok, body):
        if ok is None:
            body()
        else:
            pl.when(ok)(body)

    def started(copy, *args):
        guard(inside(*offset_of(copy, *args)), lambda: copy(*args).start())

    def offset_of(copy, *args):
        if copy is edge_copy or copy is mid_copy:
            return (args[0], 0, 0)
        if copy is col_copy:
            return (args[0], 0, 2 * args[1] - 1)
        if copy is row_copy:
            return (0, 2 * args[1] - 1, 0)
        return (0, 2 * args[1] - 1, 2 * args[2] - 1)

    for s in (2, 1):
        for k in (0, 1):
            started(edge_copy, s, k)
    for s in (2, 1, 0):
        for side in (0, 1):
            started(col_copy, s, side)
    for s in (2, 1):
        started(mid_copy, s)

    def forward(s):
        for side in (0, 1):
            started(row_copy, s, side)
        for side in (0, 1):
            edge = tile[s, edges[side], :].astype(F32)
            corner_out[s, 2 * side] = edge[0:1, :]
            corner_out[s, 2 * side + 1] = edge[broad - 1 : broad, :]
        for side in (0, 1):
            for end in (0, 1):
                started(corner_copy, s, side, end)

    forward(0)
    for s in (1, 2):

        @pl.when(t >= s)
        def _(s=s):
            for k in (0, 1):
                edge_copy(s, k).wait_recv()
            forward(s)

    along = lax.broadcasted_iota(jnp.int32, (broad, chans), 0)

    def spread(block, left, right):
        before = jnp.where(along == 0, left, pltpu.roll(block, 1, axis=0))
        after = jnp.where(along == broad - 1, right, pltpu.roll(block, broad - 1, axis=0))
        return before.astype(BF16), block.astype(BF16), after.astype(BF16)

    def dot(a, b):
        return jnp.dot(a, b, preferred_element_type=F32)

    def add_frame(s):
        for side in (0, 1):

            @pl.when(inside(0, 0, 2 * side - 1))
            def _(side=side):
                pltpu.make_async_copy(col_in.at[s, side], col_in.at[s, side], col_recv.at[s, side]).wait()

        if s > 0:
            mid_copy(s).wait_recv()
        left = jnp.where(col > 0, col_in[s, 0].astype(F32), 0.0)
        right = jnp.where(col < GRID_W - 1, col_in[s, 1].astype(F32), 0.0)
        for y in range(tall):
            rows = slice(y * broad, (y + 1) * broad)
            parts = spread(tile[s, rows, :].astype(F32), left[y : y + 1, :], right[y : y + 1, :])
            for e in range(3):
                window[rows, e * chans : (e + 1) * chans] = parts[e]
        weight_loads[s].wait()
        at = 3 * (2 - s)
        total = dot(window[...], weight[at + 1])
        if s == 0:
            acc[...] = total + bias[...].reshape(1, chans)
        else:
            acc[...] += total
        acc[broad:, :] += dot(window[:last, :], weight[at])
        acc[:last, :] += dot(window[broad:, :], weight[at + 2])

    def add_rows(s):
        for side in (0, 1):

            @pl.when(inside(0, 2 * side - 1, 0))
            def _(side=side):
                pltpu.make_async_copy(row_in.at[s, side], row_in.at[s, side], row_recv.at[s, side]).wait()
                ends = []
                for end in (0, 1):
                    k = 2 * side + end

                    @pl.when(inside(0, 0, 2 * end - 1))
                    def _(k=k):
                        pltpu.make_async_copy(corner_in.at[s, k], corner_in.at[s, k], corner_recv.at[s, k]).wait()

                    ends.append(jnp.where(inside(0, 0, 2 * end - 1), corner_in[s, k], 0.0))
                parts = spread(row_in[s, side].astype(F32), *ends)
                for e in range(3):
                    edge_window[side, :, e * chans : (e + 1) * chans] = parts[e]
                acc[edges[side], :] += dot(edge_window[side], weight[3 * (2 - s) + 2 * side])

    add_frame(0)
    for s in (1, 2):
        pl.when(t >= s)(functools.partial(add_frame, s))

        @pl.when(t < s)
        def _(s=s):
            weight_loads[s].wait()

    add_rows(0)
    for s in (1, 2):
        pl.when(t >= s)(functools.partial(add_rows, s))

    out_ref[...] = acc[...].astype(BF16)

    def sent(copy, *args):
        guard(inside(*offset_of(copy, *args)), lambda: copy(*args).wait_send())

    for s in (2, 1):
        for k in (0, 1):
            sent(edge_copy, s, k)
        sent(mid_copy, s)
    for s in (2, 1, 0):
        for side in (0, 1):
            sent(col_copy, s, side)

    def forwarded(s):
        for side in (0, 1):
            sent(row_copy, s, side)
            for end in (0, 1):
                sent(corner_copy, s, side, end)

    forwarded(0)
    for s in (1, 2):
        pl.when(t >= s)(functools.partial(forwarded, s))


def solution(mesh):
    frame_count = mesh.shape["tm"]
    tile_count = mesh.shape["tile"]

    def body(frames, norm_gain, conv_weight, conv_bias):
        _, _, tall, broad, chans = frames.shape
        pixels = tall * broad
        out = pl.pallas_call(
            functools.partial(block_kernel, tall, broad, chans, frame_count, tile_count),
            name="causal_conv",
            out_shape=pltpu.VMEM((pixels, chans), BF16),
            in_specs=[pl.BlockSpec(memory_space=pl.ANY)] * 4,
            out_specs=pl.BlockSpec(memory_space=pltpu.VMEM),
            scratch_shapes=[
                pltpu.VMEM((pixels, chans), BF16),
                pltpu.VMEM((chans,), F32),
                pltpu.VMEM((chans,), F32),
                pltpu.VMEM((9, 3 * chans, chans), BF16),
                pltpu.VMEM((3, pixels, chans), BF16),
                pltpu.VMEM((chans // LANES, pixels, LANES), F32),
                pltpu.VMEM((2, tall, chans), BF16),
                pltpu.VMEM((3, 2, tall, chans), BF16),
                pltpu.VMEM((3, 2, broad, chans), BF16),
                pltpu.VMEM((3, 4, 1, chans), F32),
                pltpu.VMEM((3, 4, 1, chans), F32),
                pltpu.VMEM((pixels, 3 * chans), BF16),
                pltpu.VMEM((2, broad, 3 * chans), BF16),
                pltpu.VMEM((pixels, chans), F32),
                pltpu.SemaphoreType.DMA((3,)),
                pltpu.SemaphoreType.DMA((3,)),
                pltpu.SemaphoreType.DMA((3, 2)),
                pltpu.SemaphoreType.DMA((3, 2)),
                pltpu.SemaphoreType.DMA((3,)),
                pltpu.SemaphoreType.DMA((3,)),
                pltpu.SemaphoreType.DMA((3, 2)),
                pltpu.SemaphoreType.DMA((3, 2)),
                pltpu.SemaphoreType.DMA((3, 2)),
                pltpu.SemaphoreType.DMA((3, 2)),
                pltpu.SemaphoreType.DMA((3, 4)),
                pltpu.SemaphoreType.DMA((3, 4)),
            ],
            compiler_params=pltpu.CompilerParams(collective_id=0, has_side_effects=True),
        )(
            frames.reshape(pixels, chans),
            norm_gain,
            conv_weight.reshape(9, 3 * chans, chans),
            conv_bias,
        )
        return out.reshape(1, 1, tall, broad, chans)

    return jax.shard_map(
        body,
        mesh=mesh,
        in_specs=(P("tm", "tile", None, None, None), P(), P(), P()),
        out_specs=P("tm", "tile", None, None, None),
        check_vma=False,
    )
```

time: 72.3 us -> 18.9 us (0.26)
  the two profiles are of different devices: /device:TPU:257 before, /device:TPU:205 now
where the time goes in v1:
time: 18.9 us; the launch traced here: 18.8 us
  Pallas kernels  18.2 us (96%)
  local copies, waits for them, and re-layouts  0.64 us (3%)
    pallas_call x1, Pallas kernels, body(): pl.pallas_call(functools.partial(block_kernel, tall, broad, chans, frame_...  18.2 us
    unnamed x1, local copies, waits for them, and re-layouts  0.64 us

profile of v1, /device:TPU:205, one launch (start us, length us, event | category | flops | bytes accessed | tf_op | source)
XLA Modules:
  0.0 18.8 jit_solution(11609868056855702682)
XLA Ops:
  0.0 18.2 %causal_conv.1 = bf16[128,384]{1,0:T(8,128)(2,1)S(1)} custom-call(bf16[128,384]{1,0:T(8,128)(2,1)} %bitcast.5, f32[384]{0:T(512)} %gain_hbm.1, bf16[9,1152,384]{2,1,0:T(8,128)(2,1)} %bitcast.4, f32[384]{0:T(512)} %bias_hbm.1), custom_call_target="tpu_custom_call" | custom-call | tf_op jit(solution)/shard_map/causal_conv/pallas_call | solution.py:327
  18.2 0.6 %copy.6 = bf16[1,1,8,16,384]{4,3,2,1,0:T(8,128)(2,1)} copy(bf16[1,1,8,16,384]{4,3,2,1,0:T(8,128)(2,1)S(1)} %bitcast.3) | data formatting | bytes 196608

commit v2 on v1

v2 whole, which is shorter than its diff:
```python
import functools

import jax
import jax.numpy as jnp
from jax import lax
from jax.experimental import pallas as pl
from jax.experimental.pallas import tpu as pltpu
from jax.sharding import PartitionSpec as P

GRID_W = 8
LANES = 128
RING_Y = 8
MESH = pl.DeviceIdType.MESH
F32 = jnp.float32
BF16 = jnp.bfloat16


def block_kernel(
    tall,
    broad,
    chans,
    frame_count,
    tile_count,
    frames_hbm,
    gain_hbm,
    weight_hbm,
    bias_hbm,
    out_ref,
    raw,
    gain,
    bias,
    weight,
    tile,
    act32,
    col_out,
    col_in,
    row_in,
    corner_out,
    corner_in,
    window,
    side_window,
    acc,
    load_sem,
    weight_sem,
    far_sem,
    edge_send,
    edge_recv,
    mid_send,
    mid_recv,
    col_send,
    col_recv,
    row_send,
    row_recv,
    corner_send,
    corner_recv,
):
    t = lax.axis_index("tm")
    i = lax.axis_index("tile")
    row = lax.div(i, GRID_W)
    col = lax.rem(i, GRID_W)
    grid_h = tile_count // GRID_W
    pixels = tall * broad
    last = pixels - broad

    loads = [
        pltpu.make_async_copy(frames_hbm, raw, load_sem.at[0]),
        pltpu.make_async_copy(gain_hbm, gain, load_sem.at[1]),
        pltpu.make_async_copy(bias_hbm, bias, load_sem.at[2]),
    ]
    for load in loads:
        load.start()

    def inside(dt, dr, dc):
        tests = []
        if dt > 0:
            tests.append(t + dt < frame_count)
        if dt < 0:
            tests.append(t + dt >= 0)
        if dr > 0:
            tests.append(row + dr < grid_h)
        if dr < 0:
            tests.append(row + dr >= 0)
        if dc > 0:
            tests.append(col + dc < GRID_W)
        if dc < 0:
            tests.append(col + dc >= 0)
        return functools.reduce(jnp.logical_and, tests)

    def signal(sem, dt, index):
        pl.semaphore_signal(sem, 1, device_id={"tm": t + dt, "tile": index}, device_id_type=MESH)

    def along_y(index, by):
        return lax.div(index, 2 * RING_Y) * 2 * RING_Y + lax.rem(index + 2 * by + 2 * RING_Y, 2 * RING_Y)

    barrier = pltpu.get_barrier_semaphore()
    count = jnp.int32(1)
    for dr in (-1, 1):
        pl.when(inside(0, dr, 0))(functools.partial(signal, barrier, 0, along_y(i + dr * GRID_W, 2)))
    signal(barrier, 0, along_y(i, 2))
    told = along_y(i, -2)
    told_row = lax.div(told, GRID_W)
    count = count + (told_row > 0).astype(jnp.int32) + (told_row < grid_h - 1).astype(jnp.int32)
    partners = [(dt, dc) for dt in (-2, 2, -1, 1, 0) for dc in (-1, 1)]
    partners += [(dt, 0) for dt in (-2, 2, -1, 1)]
    for dt, dc in partners:
        ok = inside(dt, 0, dc)
        count = count + ok.astype(jnp.int32)
        pl.when(ok)(functools.partial(signal, barrier, dt, i + dc))

    weight_loads = [
        pltpu.make_async_copy(
            weight_hbm.at[pl.ds(6 - 3 * s, 3)], weight.at[pl.ds(6 - 3 * s, 3)], weight_sem.at[s]
        )
        for s in range(3)
    ]
    for load in weight_loads:
        load.start()

    loads[0].wait()
    loads[1].wait()

    values = raw[...].astype(F32)
    scale = lax.rsqrt(jnp.mean(values * values, axis=-1, keepdims=True) + 1e-06)
    result = jax.nn.silu(values * scale * gain[...].reshape(1, chans)).astype(BF16)
    tile[0] = result
    for j in range(chans // LANES):
        lanes = slice(j * LANES, (j + 1) * LANES)
        act32[j] = result[:, lanes].astype(F32)
        for side in (0, 1):
            column = act32[j, pl.ds(side * (broad - 1), tall, stride=broad), :]
            col_out[side, :, lanes] = column.astype(BF16)

    pl.semaphore_wait(barrier, count)
    signal(far_sem, 0, told)

    def remote(src, dst, send, recv, offset):
        dt, dr, dc = offset
        return pltpu.make_async_remote_copy(
            src_ref=src,
            dst_ref=dst,
            send_sem=send,
            recv_sem=recv,
            device_id={"tm": t + dt, "tile": i + dr * GRID_W + dc},
            device_id_type=MESH,
        )

    edges = (pl.ds(0, broad), pl.ds(last, broad))
    middle = pl.ds(broad, pixels - 2 * broad)

    def edge_copy(s, k):
        offset = (s, 0, 0)
        return remote(tile.at[0, edges[k]], tile.at[s, edges[k]], edge_send.at[s, k], edge_recv.at[s, k], offset), offset

    def mid_copy(s):
        offset = (s, 0, 0)
        return remote(tile.at[0, middle], tile.at[s, middle], mid_send.at[s], mid_recv.at[s], offset), offset

    def col_copy(s, side):
        offset = (s, 0, 2 * side - 1)
        return remote(col_out.at[side], col_in.at[s, 1 - side], col_send.at[s, side], col_recv.at[s, 1 - side], offset), offset

    def row_copy(s, side):
        offset = (0, 2 * side - 1, 0)
        return remote(tile.at[s, edges[side]], row_in.at[s, 1 - side], row_send.at[s, side], row_recv.at[s, 1 - side], offset), offset

    def corner_copy(s, side):
        offset = (0, 2 * side - 1, 0)
        return remote(corner_out.at[s, side], corner_in.at[s, 1 - side], corner_send.at[s, side], corner_recv.at[s, 1 - side], offset), offset

    def start(copy, *args):
        made, offset = copy(*args)
        pl.when(inside(*offset))(made.start)

    def sent(copy, *args):
        made, offset = copy(*args)
        pl.when(inside(*offset))(made.wait_send)

    def arrived(ref, sem):
        pltpu.make_async_copy(ref, ref, sem).wait()

    for s in (2, 1):
        for k in (0, 1):
            start(edge_copy, s, k)
        for side in (0, 1):
            start(col_copy, s, side)
    for side in (0, 1):
        start(col_copy, 0, side)
    for s in (2, 1):
        start(mid_copy, s)

    pl.semaphore_wait(far_sem, 1)

    def send_rows(s):
        for side in (0, 1):
            start(row_copy, s, side)

    def send_corners(s):
        for end in (0, 1):
            pl.when(inside(0, 0, 2 * end - 1))(
                functools.partial(arrived, col_in.at[s, end], col_recv.at[s, end])
            )
        for end in (0, 1):
            column = jnp.where(inside(0, 0, 2 * end - 1), col_in[s, end].astype(F32), 0.0)
            corner_out[s, 0, end] = column[0:1, :]
            corner_out[s, 1, end] = column[tall - 1 : tall, :]
        for side in (0, 1):
            start(corner_copy, s, side)

    send_rows(0)
    send_corners(0)
    for s in (1, 2):

        @pl.when(t >= s)
        def _(s=s):
            for k in (0, 1):
                edge_copy(s, k)[0].wait_recv()
            send_rows(s)
            send_corners(s)

    along = lax.broadcasted_iota(jnp.int32, (broad, chans), 0)

    def spread(block, left, right):
        before = jnp.where(along == 0, left, pltpu.roll(block, 1, axis=0))
        after = jnp.where(along == broad - 1, right, pltpu.roll(block, broad - 1, axis=0))
        return before.astype(BF16), block.astype(BF16), after.astype(BF16)

    def dot(a, b):
        return jnp.dot(a, b, preferred_element_type=F32)

    def add_tile(s):
        if s > 0:
            mid_copy(s)[0].wait_recv()
        left, right = (
            jnp.where(inside(0, 0, 2 * end - 1), col_in[s, end].astype(F32), 0.0) for end in (0, 1)
        )
        for y in range(tall):
            rows = slice(y * broad, (y + 1) * broad)
            parts = spread(tile[s, rows, :].astype(F32), left[y : y + 1, :], right[y : y + 1, :])
            for e in range(3):
                window[rows, e * chans : (e + 1) * chans] = parts[e]
        weight_loads[s].wait()
        at = 6 - 3 * s
        total = dot(window[...], weight[at + 1])
        if s == 0:
            acc[...] = total + bias[...].reshape(1, chans)
        else:
            acc[...] += total
        acc[broad:, :] += dot(window[:last, :], weight[at])
        acc[:last, :] += dot(window[broad:, :], weight[at + 2])

    def add_rows(s):
        for side in (0, 1):

            @pl.when(inside(0, 2 * side - 1, 0))
            def _(side=side):
                arrived(row_in.at[s, side], row_recv.at[s, side])
                arrived(corner_in.at[s, side], corner_recv.at[s, side])

        for side in (0, 1):
            there = inside(0, 2 * side - 1, 0)
            halo = jnp.where(there, row_in[s, side].astype(F32), 0.0)
            ends = [
                jnp.where(jnp.logical_and(there, inside(0, 0, 2 * end - 1)), corner_in[s, side, end], 0.0)
                for end in (0, 1)
            ]
            parts = spread(halo, *ends)
            for e in range(3):
                side_window[side, :, e * chans : (e + 1) * chans] = parts[e]
        for side in (0, 1):
            acc[edges[side], :] += dot(side_window[side], weight[6 - 3 * s + 2 * side])

    loads[2].wait()
    add_tile(0)
    for s in (1, 2):
        pl.when(t >= s)(functools.partial(add_tile, s))
        pl.when(t < s)(weight_loads[s].wait)

    for s in (2, 1):
        for k in (0, 1):
            sent(edge_copy, s, k)
        sent(mid_copy, s)
    for s in (2, 1, 0):
        for side in (0, 1):
            sent(col_copy, s, side)

    def forwarded(s):
        for side in (0, 1):
            sent(row_copy, s, side)
            sent(corner_copy, s, side)

    forwarded(0)
    for s in (1, 2):
        pl.when(t >= s)(functools.partial(forwarded, s))

    inner = slice(broad, last)
    out_ref[inner, :] = acc[inner, :].astype(BF16)
    add_rows(0)
    for s in (1, 2):
        pl.when(t >= s)(functools.partial(add_rows, s))
    for side in (0, 1):
        out_ref[edges[side], :] = acc[edges[side], :].astype(BF16)


def solution(mesh):
    frame_count = mesh.shape["tm"]
    tile_count = mesh.shape["tile"]

    def body(frames, norm_gain, conv_weight, conv_bias):
        _, _, tall, broad, chans = frames.shape
        pixels = tall * broad
        out = pl.pallas_call(
            functools.partial(block_kernel, tall, broad, chans, frame_count, tile_count),
            name="causal_conv",
            out_shape=pltpu.VMEM((pixels, chans), BF16),
            in_specs=[pl.BlockSpec(memory_space=pl.ANY)] * 4,
            out_specs=pl.BlockSpec(memory_space=pltpu.VMEM),
            scratch_shapes=[
                pltpu.VMEM((pixels, chans), BF16),
                pltpu.VMEM((chans,), F32),
                pltpu.VMEM((chans,), F32),
                pltpu.VMEM((9, 3 * chans, chans), BF16),
                pltpu.VMEM((3, pixels, chans), BF16),
                pltpu.VMEM((chans // LANES, pixels, LANES), F32),
                pltpu.VMEM((2, tall, chans), BF16),
                pltpu.VMEM((3, 2, tall, chans), BF16),
                pltpu.VMEM((3, 2, broad, chans), BF16),
                pltpu.VMEM((3, 2, 2, 1, chans), F32),
                pltpu.VMEM((3, 2, 2, 1, chans), F32),
                pltpu.VMEM((pixels, 3 * chans), BF16),
                pltpu.VMEM((2, broad, 3 * chans), BF16),
                pltpu.VMEM((pixels, chans), F32),
                pltpu.SemaphoreType.DMA((3,)),
                pltpu.SemaphoreType.DMA((3,)),
                pltpu.SemaphoreType.REGULAR,
                pltpu.SemaphoreType.DMA((3, 2)),
                pltpu.SemaphoreType.DMA((3, 2)),
                pltpu.SemaphoreType.DMA((3,)),
                pltpu.SemaphoreType.DMA((3,)),
                pltpu.SemaphoreType.DMA((3, 2)),
                pltpu.SemaphoreType.DMA((3, 2)),
                pltpu.SemaphoreType.DMA((3, 2)),
                pltpu.SemaphoreType.DMA((3, 2)),
                pltpu.SemaphoreType.DMA((3, 2)),
                pltpu.SemaphoreType.DMA((3, 2)),
            ],
            compiler_params=pltpu.CompilerParams(collective_id=0, has_side_effects=True),
        )(
            frames.reshape(pixels, chans),
            norm_gain,
            conv_weight.reshape(9, 3 * chans, chans),
            conv_bias,
        )
        return out.reshape(1, 1, tall, broad, chans)

    return jax.shard_map(
        body,
        mesh=mesh,
        in_specs=(P("tm", "tile", None, None, None), P(), P(), P()),
        out_specs=P("tm", "tile", None, None, None),
        check_vma=False,
    )
```

time: 18.9 us -> 17.6 us (0.931)
  the two profiles are of different devices: /device:TPU:205 before, /device:TPU:246 now
where the time goes in v2:
time: 17.6 us; the launch traced here: 17.5 us
  Pallas kernels  16.8 us (95%)
  local copies, waits for them, and re-layouts  0.64 us (4%)
    pallas_call x1, Pallas kernels, body(): pl.pallas_call(functools.partial(block_kernel, tall, broad, chans, frame_...  16.8 us
    unnamed x1, local copies, waits for them, and re-layouts  0.64 us

profile of v2, /device:TPU:246, one launch (start us, length us, event | category | flops | bytes accessed | tf_op | source)
XLA Modules:
  0.0 17.5 jit_solution(10364142462594539441)
XLA Ops:
  0.0 16.8 %causal_conv.1 = bf16[128,384]{1,0:T(8,128)(2,1)S(1)} custom-call(bf16[128,384]{1,0:T(8,128)(2,1)} %bitcast.5, f32[384]{0:T(512)} %gain_hbm.1, bf16[9,1152,384]{2,1,0:T(8,128)(2,1)} %bitcast.4, f32[384]{0:T(512)} %bias_hbm.1), custom_call_target="tpu_custom_call" | custom-call | tf_op jit(solution)/shard_map/causal_conv/pallas_call | solution.py:311
  16.8 0.6 %copy.6 = bf16[1,1,8,16,384]{4,3,2,1,0:T(8,128)(2,1)} copy(bf16[1,1,8,16,384]{4,3,2,1,0:T(8,128)(2,1)S(1)} %bitcast.3) | data formatting | bytes 196608

commit v3 on v2

v3 whole, which is shorter than its diff:
```python
import functools

import jax
import jax.numpy as jnp
from jax import lax
from jax.experimental import pallas as pl
from jax.experimental.pallas import tpu as pltpu
from jax.sharding import PartitionSpec as P

GRID_W = 8
LANES = 128
MESH = pl.DeviceIdType.MESH
F32 = jnp.float32
BF16 = jnp.bfloat16


def block_kernel(
    tall,
    broad,
    chans,
    frame_count,
    tile_count,
    frames_hbm,
    gain_hbm,
    weight_hbm,
    bias_hbm,
    out_ref,
    raw,
    gain,
    bias,
    weight,
    tile,
    act32,
    col_out,
    col_in,
    corner_out,
    corner_in,
    part_out,
    part_in,
    window,
    acc,
    part,
    load_sem,
    weight_sem,
    far_sem,
    tile_send,
    edge_recv,
    mid_recv,
    side_send,
    corner_recv,
    col_recv,
    part_send,
    part_recv,
):
    t = lax.axis_index("tm")
    i = lax.axis_index("tile")
    row = lax.div(i, GRID_W)
    col = lax.rem(i, GRID_W)
    grid_h = tile_count // GRID_W
    pixels = tall * broad
    last = pixels - broad
    half = lax.rem(row, 2)

    loads = [
        pltpu.make_async_copy(frames_hbm, raw, load_sem.at[0]),
        pltpu.make_async_copy(gain_hbm, gain, load_sem.at[1]),
        pltpu.make_async_copy(bias_hbm, bias, load_sem.at[1]),
    ]
    for load in loads:
        load.start()

    def inside(dt, dr, dc):
        tests = []
        if dt > 0:
            tests.append(t + dt < frame_count)
        if dt < 0:
            tests.append(t + dt >= 0)
        if dr > 0:
            tests.append(row + dr < grid_h)
        if dr < 0:
            tests.append(row + dr >= 0)
        if dc > 0:
            tests.append(col + dc < GRID_W)
        if dc < 0:
            tests.append(col + dc >= 0)
        return functools.reduce(jnp.logical_and, tests)

    def signal(sem, dt, index):
        pl.semaphore_signal(sem, 1, device_id={"tm": t + dt, "tile": index}, device_id_type=MESH)

    barrier = pltpu.get_barrier_semaphore()
    partners = [(dt, dc) for dt in (-2, 2) for dc in (-1, 1)]
    partners += [(dt, 0) for dt in (-2, 2)]
    partners += [(dt, dc) for dt in (-1, 1, 0) for dc in (-1, 1)]
    partners += [(dt, 0) for dt in (-1, 1)]
    beyond = jnp.logical_and(half == 1, row < grid_h - 1)
    signal(barrier, 0, i + GRID_W // 2 * (1 - 2 * half))
    signal(barrier, 0, jnp.where(beyond, i + 3 * GRID_W // 2, i))
    for dt, dc in partners:
        ok = inside(dt, 0, dc)
        signal(barrier, jnp.where(ok, dt, 0), jnp.where(ok, i + dc, i))
    place = lax.rem(i, 2 * GRID_W)
    half_way = jnp.logical_and(place >= GRID_W // 2, place < 3 * GRID_W // 2)
    above = i >= 2 * GRID_W
    met = 2 + above.astype(jnp.int32)
    count = len(partners) + jnp.logical_not(beyond).astype(jnp.int32) + jnp.where(half_way, met, 0)

    weight_loads = [
        pltpu.make_async_copy(
            weight_hbm.at[pl.ds(6 - 3 * s, 3)], weight.at[pl.ds(6 - 3 * s, 3)], weight_sem.at[0]
        )
        for s in range(3)
    ]
    for load in weight_loads:
        load.start()

    def arrived(ref, sem):
        pltpu.make_async_copy(ref, ref, sem).wait()

    loads[0].wait()
    arrived(corner_in.at[pl.ds(0, 2)], load_sem.at[1])

    values = raw[...].astype(F32)
    scale = lax.rsqrt(jnp.mean(values * values, axis=-1, keepdims=True) + 1e-06)
    result = jax.nn.silu(values * scale * gain[...].reshape(1, chans)).astype(BF16)
    tile[0, :broad, :] = result[:broad]
    tile[0, broad : 2 * broad, :] = result[last:]
    tile[0, 2 * broad :, :] = result[broad:last]
    for j in range(chans // LANES):
        lanes = slice(j * LANES, (j + 1) * LANES)
        act32[j] = result[:, lanes].astype(F32)
        for side in (0, 1):
            column = act32[j, pl.ds(side * (broad - 1), tall, stride=broad), :]
            col_out[side, :, lanes] = column.astype(BF16)
            corner_out[2 * side, :, lanes] = column[0:1, :]
            corner_out[2 * side + 1, :, lanes] = column[tall - 1 : tall, :]

    pl.semaphore_wait(barrier, count)

    @pl.when(half_way)
    def _():
        for by in (-GRID_W // 2, GRID_W // 2):
            signal(far_sem, 0, i + by)
        pl.when(above)(functools.partial(signal, far_sem, 0, i - 3 * GRID_W // 2))


    def remote(src, dst, send, recv, offset):
        dt, dr, dc = offset
        return pltpu.make_async_remote_copy(
            src_ref=src,
            dst_ref=dst,
            send_sem=send,
            recv_sem=recv,
            device_id={"tm": t + dt, "tile": i + dr * GRID_W + dc},
            device_id_type=MESH,
        )

    edges = pl.ds(0, 2 * broad)
    middle = pl.ds(2 * broad, pixels - 2 * broad)

    def edge_copy(s):
        offset = (s, 0, 0)
        return remote(tile.at[0, edges], tile.at[s, edges], tile_send.at[s - 1], edge_recv.at[s - 1], offset), offset

    def mid_copy(s):
        offset = (s, 0, 0)
        return remote(tile.at[0, middle], tile.at[s, middle], tile_send.at[s - 1], mid_recv.at[s - 1], offset), offset

    def col_copy(s, side):
        offset = (s, 0, 2 * side - 1)
        return remote(col_out.at[side], col_in.at[s, 1 - side], side_send.at[s, side], col_recv.at[s, 1 - side], offset), offset

    def corners(s, end):
        return pl.ds(4 * (s - 1) + 2 * end, 2)

    def corner_copy(s, side):
        offset = (s, 0, 2 * side - 1)
        return remote(
            corner_out.at[pl.ds(2 * side, 2)],
            corner_in.at[corners(s, 1 - side)],
            side_send.at[s, side],
            corner_recv.at[s - 1, 1 - side],
            offset,
        ), offset

    def part_copy(side):
        offset = (0, 2 * side - 1, 0)
        return remote(part_out.at[side], part_in.at[1 - side], part_send.at[side], part_recv.at[1 - side], offset), offset

    def start(copy, *args):
        made, offset = copy(*args)
        pl.when(inside(*offset))(made.start)

    for s in (2, 1):
        for side in (0, 1):
            start(corner_copy, s, side)
        start(edge_copy, s)
    for side in (0, 1):
        start(col_copy, 0, side)
    for s in (2, 1):
        for side in (0, 1):
            start(col_copy, s, side)
    for s in (2, 1):
        start(mid_copy, s)

    along = lax.broadcasted_iota(jnp.int32, (broad, chans), 0)

    def dot(a, b):
        return jnp.dot(a, b, preferred_element_type=F32)

    def spread(ref, to, s, y, beside):
        slot = {0: 0, tall - 1: 1}.get(y, y + 1)
        block = tile[s, slot * broad : (slot + 1) * broad, :].astype(F32)
        left, right = (jnp.where(inside(0, 0, 2 * end - 1), beside[end], 0.0) for end in (0, 1))
        before = jnp.where(along == 0, left, pltpu.roll(block, 1, axis=0))
        after = jnp.where(along == broad - 1, right, pltpu.roll(block, broad - 1, axis=0))
        taps = [value.astype(BF16) for value in (before, block, after)]
        if ref is None:
            return jnp.concatenate(taps, axis=1)
        for e in range(3):
            ref[to : to + broad, e * chans : (e + 1) * chans] = taps[e]

    def wait_columns(s):
        for end in (0, 1):
            pl.when(inside(0, 0, 2 * end - 1))(
                functools.partial(arrived, col_in.at[s, end], col_recv.at[s, end])
            )

    def add_part(s):
        sums = []
        for side, y in ((0, 0), (1, tall - 1)):
            if s == 0:
                beside = [col_in[0, end, y : y + 1, :].astype(F32) for end in (0, 1)]
            else:
                beside = [corner_in[4 * (s - 1) + 2 * end + side] for end in (0, 1)]
            sums.append(dot(spread(None, None, s, y, beside), weight[8 - 3 * s - 2 * side]))
        above, below = sums
        if s == 0:
            part[0] = above
            part[1] = below
        else:
            part[0] += above
            part[1] += below

    def add_tile(s):
        for y in range(tall):
            spread(window, y * broad, s, y, [col_in[s, end, y : y + 1, :].astype(F32) for end in (0, 1)])
        at = 6 - 3 * s
        total = dot(window[...], weight[at + 1])
        if s == 0:
            acc[...] = total + bias[...].reshape(1, chans)
        else:
            acc[...] += total
        acc[broad:, :] += dot(window[:last, :], weight[at])
        acc[:last, :] += dot(window[broad:, :], weight[at + 2])

    wait_columns(0)
    arrived(weight, weight_sem.at[0])
    add_part(0)
    for s in (1, 2):

        @pl.when(t >= s)
        def _(s=s):
            arrived(tile.at[s, edges], edge_recv.at[s - 1])
            for end in (0, 1):
                pl.when(inside(0, 0, 2 * end - 1))(
                    functools.partial(arrived, corner_in.at[corners(s, end)], corner_recv.at[s - 1, end])
                )
            add_part(s)

    part_out[...] = part[...].astype(BF16)
    pl.semaphore_wait(far_sem, 1 + beyond.astype(jnp.int32))
    for side in (0, 1):
        start(part_copy, side)

    add_tile(0)
    for s in (1, 2):

        @pl.when(t >= s)
        def _(s=s):
            wait_columns(s)
            arrived(tile.at[s, middle], mid_recv.at[s - 1])
            add_tile(s)

    inner = slice(broad, last)
    out_ref[inner, :] = acc[inner, :].astype(BF16)

    def sent(ref, sem, offset):
        pl.when(inside(*offset))(functools.partial(arrived, ref, sem))

    for s in (1, 2):
        sent(tile.at[0], tile_send.at[s - 1], (s, 0, 0))
    for side in (0, 1):
        sent(col_out.at[side], side_send.at[0, side], (0, 0, 2 * side - 1))
        for s in (1, 2):
            sent(corner_in.at[pl.ds(0, 2 + tall // 2)], side_send.at[s, side], (s, 0, 2 * side - 1))
        sent(part_out.at[side], part_send.at[side], (0, 2 * side - 1, 0))

    for side in (0, 1):
        there = inside(0, 2 * side - 1, 0)
        rows = slice(side * last, side * last + broad)
        pl.when(there)(functools.partial(arrived, part_in.at[side], part_recv.at[side]))
        halo = jnp.where(there, part_in[side].astype(F32), 0.0)
        out_ref[rows, :] = (acc[rows, :] + halo).astype(BF16)


def solution(mesh):
    frame_count = mesh.shape["tm"]
    tile_count = mesh.shape["tile"]

    def body(frames, norm_gain, conv_weight, conv_bias):
        _, _, tall, broad, chans = frames.shape
        pixels = tall * broad
        out = pl.pallas_call(
            functools.partial(block_kernel, tall, broad, chans, frame_count, tile_count),
            name="causal_conv",
            out_shape=pltpu.VMEM((pixels, chans), BF16),
            in_specs=[pl.BlockSpec(memory_space=pl.ANY)] * 4,
            out_specs=pl.BlockSpec(memory_space=pltpu.VMEM),
            scratch_shapes=[
                pltpu.VMEM((pixels, chans), BF16),
                pltpu.VMEM((chans,), F32),
                pltpu.VMEM((chans,), F32),
                pltpu.VMEM((9, 3 * chans, chans), BF16),
                pltpu.VMEM((3, pixels, chans), BF16),
                pltpu.VMEM((chans // LANES, pixels, LANES), F32),
                pltpu.VMEM((2, tall, chans), BF16),
                pltpu.VMEM((3, 2, tall, chans), BF16),
                pltpu.VMEM((4, 1, chans), F32),
                pltpu.VMEM((8, 1, chans), F32),
                pltpu.VMEM((2, broad, chans), BF16),
                pltpu.VMEM((2, broad, chans), BF16),
                pltpu.VMEM((pixels, 3 * chans), BF16),
                pltpu.VMEM((pixels, chans), F32),
                pltpu.VMEM((2, broad, chans), F32),
                pltpu.SemaphoreType.DMA((2,)),
                pltpu.SemaphoreType.DMA((1,)),
                pltpu.SemaphoreType.REGULAR,
                pltpu.SemaphoreType.DMA((2,)),
                pltpu.SemaphoreType.DMA((2,)),
                pltpu.SemaphoreType.DMA((2,)),
                pltpu.SemaphoreType.DMA((3, 2)),
                pltpu.SemaphoreType.DMA((2, 2)),
                pltpu.SemaphoreType.DMA((3, 2)),
                pltpu.SemaphoreType.DMA((2,)),
                pltpu.SemaphoreType.DMA((2,)),
            ],
            compiler_params=pltpu.CompilerParams(collective_id=0, has_side_effects=True),
        )(
            frames.reshape(pixels, chans),
            norm_gain,
            conv_weight.reshape(9, 3 * chans, chans),
            conv_bias,
        )
        return out.reshape(1, 1, tall, broad, chans)

    return jax.shard_map(
        body,
        mesh=mesh,
        in_specs=(P("tm", "tile", None, None, None), P(), P(), P()),
        out_specs=P("tm", "tile", None, None, None),
        check_vma=False,
    )
```

time: 17.6 us -> 16.7 us (0.949)
  the two profiles are of different devices: /device:TPU:246 before, /device:TPU:252 now
where the time goes in v3:
time: 16.7 us; the launch traced here: 16.6 us
  Pallas kernels  15.9 us (95%)
  local copies, waits for them, and re-layouts  0.64 us (4%)
    pallas_call x1, Pallas kernels, body(): pl.pallas_call(functools.partial(block_kernel, tall, broad, chans, frame_...  15.9 us
    unnamed x1, local copies, waits for them, and re-layouts  0.64 us

profile of v3, /device:TPU:252, one launch (start us, length us, event | category | flops | bytes accessed | tf_op | source)
XLA Modules:
  0.0 16.6 jit_solution(6455854597920256601)
XLA Ops:
  0.0 15.9 %causal_conv.1 = bf16[128,384]{1,0:T(8,128)(2,1)S(1)} custom-call(bf16[128,384]{1,0:T(8,128)(2,1)} %bitcast.5, f32[384]{0:T(512)} %gain_hbm.1, bf16[9,1152,384]{2,1,0:T(8,128)(2,1)} %bitcast.4, f32[384]{0:T(512)} %bias_hbm.1), custom_call_target="tpu_custom_call" | custom-call | tf_op jit(solution)/shard_map/causal_conv/pallas_call | solution.py:314
  15.9 0.6 %copy.6 = bf16[1,1,8,16,384]{4,3,2,1,0:T(8,128)(2,1)} copy(bf16[1,1,8,16,384]{4,3,2,1,0:T(8,128)(2,1)S(1)} %bitcast.3) | data formatting | bytes 196608

commit v4 on v3

--- a/solution.py
+++ b/solution.py
@@ -93,17 +93,21 @@
     partners += [(dt, 0) for dt in (-2, 2)]
     partners += [(dt, dc) for dt in (-1, 1, 0) for dc in (-1, 1)]
     partners += [(dt, 0) for dt in (-1, 1)]
-    beyond = jnp.logical_and(half == 1, row < grid_h - 1)
-    signal(barrier, 0, i + GRID_W // 2 * (1 - 2 * half))
-    signal(barrier, 0, jnp.where(beyond, i + 3 * GRID_W // 2, i))
+    odd = half == 1
+    beyond = jnp.logical_and(odd, row < grid_h - 1)
+    above = i >= 2 * GRID_W
+    step = GRID_W // 2
+    place = lax.rem(i, 2 * GRID_W)
+    half_way = jnp.logical_and(place >= step, place < 3 * step)
+    signal(barrier, 0, jnp.where(odd, i - step, i + step))
+    signal(barrier, 0, jnp.where(odd, jnp.where(beyond, i + 3 * step, i), jnp.where(above, i + 2 * step, i)))
+    signal(barrier, 0, jnp.where(beyond, i + 4 * step, i))
     for dt, dc in partners:
         ok = inside(dt, 0, dc)
         signal(barrier, jnp.where(ok, dt, 0), jnp.where(ok, i + dc, i))
-    place = lax.rem(i, 2 * GRID_W)
-    half_way = jnp.logical_and(place >= GRID_W // 2, place < 3 * GRID_W // 2)
-    above = i >= 2 * GRID_W
-    met = 2 + above.astype(jnp.int32)
-    count = len(partners) + jnp.logical_not(beyond).astype(jnp.int32) + jnp.where(half_way, met, 0)
+    count = len(partners) + jnp.where(odd, 0, jnp.where(above, 1, 2)) + jnp.where(jnp.logical_and(odd, jnp.logical_not(beyond)), 2, 0)
+    count += jnp.where(half_way, 2 + above.astype(jnp.int32), 0)
+    count += jnp.where(jnp.logical_and(odd, above), 2, 0)
 
     weight_loads = [
         pltpu.make_async_copy(
@@ -137,12 +141,9 @@
 
     pl.semaphore_wait(barrier, count)
 
-    @pl.when(half_way)
-    def _():
-        for by in (-GRID_W // 2, GRID_W // 2):
-            signal(far_sem, 0, i + by)
-        pl.when(above)(functools.partial(signal, far_sem, 0, i - 3 * GRID_W // 2))
-
+    pl.when(half_way)(functools.partial(signal, far_sem, 0, i - step))
+    pl.when(jnp.logical_and(half_way, jnp.logical_not(above)))(functools.partial(signal, far_sem, 0, i + step))
+    pl.when(jnp.logical_and(odd, above))(functools.partial(signal, far_sem, 0, i - 4 * step))
 
     def remote(src, dst, send, recv, offset):
         dt, dr, dc = offset
@@ -191,17 +192,12 @@
         made, offset = copy(*args)
         pl.when(inside(*offset))(made.start)
 
-    for s in (2, 1):
+    for s in (1, 2):
         for side in (0, 1):
             start(corner_copy, s, side)
         start(edge_copy, s)
     for side in (0, 1):
         start(col_copy, 0, side)
-    for s in (2, 1):
-        for side in (0, 1):
-            start(col_copy, s, side)
-    for s in (2, 1):
-        start(mid_copy, s)
 
     along = lax.broadcasted_iota(jnp.int32, (broad, chans), 0)
 
@@ -258,6 +254,11 @@
     arrived(weight, weight_sem.at[0])
     add_part(0)
     for s in (1, 2):
+        for side in (0, 1):
+            start(col_copy, s, side)
+        start(mid_copy, s)
+
+    for s in (1, 2):
 
         @pl.when(t >= s)
         def _(s=s):
@@ -269,7 +270,8 @@
             add_part(s)
 
     part_out[...] = part[...].astype(BF16)
-    pl.semaphore_wait(far_sem, 1 + beyond.astype(jnp.int32))
+    told = jnp.where(odd, beyond.astype(jnp.int32) + jnp.logical_not(above).astype(jnp.int32), 1)
+    pl.when(told > 0)(functools.partial(pl.semaphore_wait, far_sem, told))
     for side in (0, 1):
         start(part_copy, side)
 

time: 16.7 us -> 16.2 us (0.970)
  the two profiles are of different devices: /device:TPU:252 before, /device:TPU:192 now
where the time goes in v4:
time: 16.2 us; the launch traced here: 16.1 us
  Pallas kernels  15.4 us (95%)
  local copies, waits for them, and re-layouts  0.64 us (4%)
    pallas_call x1, Pallas kernels, body(): pl.pallas_call(functools.partial(block_kernel, tall, broad, chans, frame_...  15.4 us
    unnamed x1, local copies, waits for them, and re-layouts  0.64 us

profile of v4, /device:TPU:192, one launch (start us, length us, event | category | flops | bytes accessed | tf_op | source)
XLA Modules:
  0.0 16.1 jit_solution(14013213736530361229)
XLA Ops:
  0.0 15.4 %causal_conv.1 = bf16[128,384]{1,0:T(8,128)(2,1)S(1)} custom-call(bf16[128,384]{1,0:T(8,128)(2,1)} %bitcast.5, f32[384]{0:T(512)} %gain_hbm.1, bf16[9,1152,384]{2,1,0:T(8,128)(2,1)} %bitcast.4, f32[384]{0:T(512)} %bias_hbm.1), custom_call_target="tpu_custom_call" | custom-call | tf_op jit(solution)/shard_map/causal_conv/pallas_call | solution.py:316
  15.4 0.6 %copy.6 = bf16[1,1,8,16,384]{4,3,2,1,0:T(8,128)(2,1)} copy(bf16[1,1,8,16,384]{4,3,2,1,0:T(8,128)(2,1)S(1)} %bitcast.3) | data formatting | bytes 196608

commit v5 on v4

--- a/solution.py
+++ b/solution.py
@@ -40,16 +40,16 @@
     window,
     acc,
     part,
+    measure,
     load_sem,
     weight_sem,
     far_sem,
     tile_send,
+    side_send,
+    part_send,
     edge_recv,
-    mid_recv,
-    side_send,
-    corner_recv,
+    rest_recv,
     col_recv,
-    part_send,
     part_recv,
 ):
     t = lax.axis_index("tm")
@@ -121,8 +121,18 @@
     def arrived(ref, sem):
         pltpu.make_async_copy(ref, ref, sem).wait()
 
+    def took(pixels_f32, sem):
+        arrived(measure.at[pl.ds(0, pixels_f32)], sem)
+
+    both_sides = jnp.logical_and(col > 0, col < GRID_W - 1)
+    both_rows = jnp.logical_and(row > 0, row < grid_h - 1)
+
+    def took_sides(base, each, sem):
+        pl.when(both_sides)(functools.partial(took, base + 2 * each, sem))
+        pl.when(jnp.logical_not(both_sides))(functools.partial(took, base + each, sem))
+
     loads[0].wait()
-    arrived(corner_in.at[pl.ds(0, 2)], load_sem.at[1])
+    took(2, load_sem.at[1])
 
     values = raw[...].astype(F32)
     scale = lax.rsqrt(jnp.mean(values * values, axis=-1, keepdims=True) + 1e-06)
@@ -161,15 +171,16 @@
 
     def edge_copy(s):
         offset = (s, 0, 0)
-        return remote(tile.at[0, edges], tile.at[s, edges], tile_send.at[s - 1], edge_recv.at[s - 1], offset), offset
+        return remote(tile.at[0, edges], tile.at[s, edges], tile_send.at[0], edge_recv.at[s - 1], offset), offset
 
     def mid_copy(s):
         offset = (s, 0, 0)
-        return remote(tile.at[0, middle], tile.at[s, middle], tile_send.at[s - 1], mid_recv.at[s - 1], offset), offset
+        return remote(tile.at[0, middle], tile.at[s, middle], tile_send.at[0], rest_recv.at[s - 1], offset), offset
 
     def col_copy(s, side):
         offset = (s, 0, 2 * side - 1)
-        return remote(col_out.at[side], col_in.at[s, 1 - side], side_send.at[s, side], col_recv.at[s, 1 - side], offset), offset
+        recv = rest_recv.at[s - 1] if s else col_recv.at[0]
+        return remote(col_out.at[side], col_in.at[s, 1 - side], side_send.at[side], recv, offset), offset
 
     def corners(s, end):
         return pl.ds(4 * (s - 1) + 2 * end, 2)
@@ -179,14 +190,14 @@
         return remote(
             corner_out.at[pl.ds(2 * side, 2)],
             corner_in.at[corners(s, 1 - side)],
-            side_send.at[s, side],
-            corner_recv.at[s - 1, 1 - side],
+            side_send.at[side],
+            edge_recv.at[s - 1],
             offset,
         ), offset
 
     def part_copy(side):
         offset = (0, 2 * side - 1, 0)
-        return remote(part_out.at[side], part_in.at[1 - side], part_send.at[side], part_recv.at[1 - side], offset), offset
+        return remote(part_out.at[side], part_in.at[1 - side], part_send.at[0], part_recv.at[0], offset), offset
 
     def start(copy, *args):
         made, offset = copy(*args)
@@ -215,12 +226,6 @@
             return jnp.concatenate(taps, axis=1)
         for e in range(3):
             ref[to : to + broad, e * chans : (e + 1) * chans] = taps[e]
-
-    def wait_columns(s):
-        for end in (0, 1):
-            pl.when(inside(0, 0, 2 * end - 1))(
-                functools.partial(arrived, col_in.at[s, end], col_recv.at[s, end])
-            )
 
     def add_part(s):
         sums = []
@@ -250,7 +255,7 @@
         acc[broad:, :] += dot(window[:last, :], weight[at])
         acc[:last, :] += dot(window[broad:, :], weight[at + 2])
 
-    wait_columns(0)
+    took_sides(0, tall // 2, col_recv.at[0])
     arrived(weight, weight_sem.at[0])
     add_part(0)
     for s in (1, 2):
@@ -262,46 +267,46 @@
 
         @pl.when(t >= s)
         def _(s=s):
-            arrived(tile.at[s, edges], edge_recv.at[s - 1])
-            for end in (0, 1):
-                pl.when(inside(0, 0, 2 * end - 1))(
-                    functools.partial(arrived, corner_in.at[corners(s, end)], corner_recv.at[s - 1, end])
-                )
+            took_sides(broad, 2, edge_recv.at[s - 1])
             add_part(s)
 
     part_out[...] = part[...].astype(BF16)
+    greeted = jnp.logical_and(odd, above)
+    up = part_copy(0)[0]
+    pl.when(greeted)(up.start)
     told = jnp.where(odd, beyond.astype(jnp.int32) + jnp.logical_not(above).astype(jnp.int32), 1)
     pl.when(told > 0)(functools.partial(pl.semaphore_wait, far_sem, told))
-    for side in (0, 1):
-        start(part_copy, side)
+    pl.when(jnp.logical_and(inside(0, -1, 0), jnp.logical_not(greeted)))(up.start)
+    start(part_copy, 1)
 
     add_tile(0)
     for s in (1, 2):
 
         @pl.when(t >= s)
         def _(s=s):
-            wait_columns(s)
-            arrived(tile.at[s, middle], mid_recv.at[s - 1])
+            took_sides((pixels - 2 * broad) // 2, tall // 2, rest_recv.at[s - 1])
             add_tile(s)
 
     inner = slice(broad, last)
     out_ref[inner, :] = acc[inner, :].astype(BF16)
 
-    def sent(ref, sem, offset):
-        pl.when(inside(*offset))(functools.partial(arrived, ref, sem))
-
-    for s in (1, 2):
-        sent(tile.at[0], tile_send.at[s - 1], (s, 0, 0))
+    pl.when(t < frame_count - 2)(functools.partial(arrived, tile.at[pl.ds(0, 2)], tile_send.at[0]))
+    pl.when(t == frame_count - 2)(functools.partial(arrived, tile.at[0], tile_send.at[0]))
     for side in (0, 1):
-        sent(col_out.at[side], side_send.at[0, side], (0, 0, 2 * side - 1))
-        for s in (1, 2):
-            sent(corner_in.at[pl.ds(0, 2 + tall // 2)], side_send.at[s, side], (s, 0, 2 * side - 1))
-        sent(part_out.at[side], part_send.at[side], (0, 2 * side - 1, 0))
-
+        there = inside(0, 0, 2 * side - 1)
+        for later in range(3):
+            holds = t == frame_count - 1 - later if later < 2 else t < frame_count - 2
+            pl.when(jnp.logical_and(there, holds))(
+                functools.partial(took, tall // 2 + later * (tall // 2 + 2), side_send.at[side])
+            )
+    pl.when(both_rows)(functools.partial(arrived, part_out, part_send.at[0]))
+    pl.when(jnp.logical_not(both_rows))(functools.partial(arrived, part_out.at[0], part_send.at[0]))
+
+    pl.when(both_rows)(functools.partial(arrived, part_in, part_recv.at[0]))
+    pl.when(jnp.logical_not(both_rows))(functools.partial(arrived, part_in.at[0], part_recv.at[0]))
     for side in (0, 1):
         there = inside(0, 2 * side - 1, 0)
         rows = slice(side * last, side * last + broad)
-        pl.when(there)(functools.partial(arrived, part_in.at[side], part_recv.at[side]))
         halo = jnp.where(there, part_in[side].astype(F32), 0.0)
         out_ref[rows, :] = (acc[rows, :] + halo).astype(BF16)
 
@@ -335,17 +340,17 @@
                 pltpu.VMEM((pixels, 3 * chans), BF16),
                 pltpu.VMEM((pixels, chans), F32),
                 pltpu.VMEM((2, broad, chans), F32),
+                pltpu.VMEM(((pixels - 2 * broad) // 2 + tall, 1, chans), F32),
                 pltpu.SemaphoreType.DMA((2,)),
                 pltpu.SemaphoreType.DMA((1,)),
                 pltpu.SemaphoreType.REGULAR,
+                pltpu.SemaphoreType.DMA((1,)),
+                pltpu.SemaphoreType.DMA((2,)),
+                pltpu.SemaphoreType.DMA((1,)),
                 pltpu.SemaphoreType.DMA((2,)),
                 pltpu.SemaphoreType.DMA((2,)),
-                pltpu.SemaphoreType.DMA((2,)),
-                pltpu.SemaphoreType.DMA((3, 2)),
-                pltpu.SemaphoreType.DMA((2, 2)),
-                pltpu.SemaphoreType.DMA((3, 2)),
-                pltpu.SemaphoreType.DMA((2,)),
-                pltpu.SemaphoreType.DMA((2,)),
+                pltpu.SemaphoreType.DMA((1,)),
+                pltpu.SemaphoreType.DMA((1,)),
             ],
             compiler_params=pltpu.CompilerParams(collective_id=0, has_side_effects=True),
         )(

time: 16.2 us -> 15.7 us (0.969)
  the two profiles are of different devices: /device:TPU:192 before, /device:TPU:244 now
where the time goes in v5:
time: 15.7 us; the launch traced here: 15.6 us
  Pallas kernels  15 us (96%)
  local copies, waits for them, and re-layouts  0.64 us (4%)
    pallas_call x1, Pallas kernels, body(): pl.pallas_call(functools.partial(block_kernel, tall, broad, chans, frame_...  15 us
    unnamed x1, local copies, waits for them, and re-layouts  0.64 us

profile of v5, /device:TPU:244, one launch (start us, length us, event | category | flops | bytes accessed | tf_op | source)
XLA Modules:
  0.0 15.6 jit_solution(90098041785023547)
XLA Ops:
  0.0 15.0 %causal_conv.1 = bf16[128,384]{1,0:T(8,128)(2,1)S(1)} custom-call(bf16[128,384]{1,0:T(8,128)(2,1)} %bitcast.5, f32[384]{0:T(512)} %gain_hbm.1, bf16[9,1152,384]{2,1,0:T(8,128)(2,1)} %bitcast.4, f32[384]{0:T(512)} %bias_hbm.1), custom_call_target="tpu_custom_call" | custom-call | tf_op jit(solution)/shard_map/causal_conv/pallas_call | solution.py:321
  15.0 0.6 %copy.6 = bf16[1,1,8,16,384]{4,3,2,1,0:T(8,128)(2,1)} copy(bf16[1,1,8,16,384]{4,3,2,1,0:T(8,128)(2,1)S(1)} %bitcast.3) | data formatting | bytes 196608

commit v6 on v5

--- a/solution.py
+++ b/solution.py
@@ -227,21 +227,29 @@
         for e in range(3):
             ref[to : to + broad, e * chans : (e + 1) * chans] = taps[e]
 
+    told = jnp.where(odd, beyond.astype(jnp.int32) + jnp.logical_not(above).astype(jnp.int32), 1)
+
+    def add_side(s, side):
+        y = side * (tall - 1)
+        if s == 0:
+            beside = [col_in[0, end, y : y + 1, :].astype(F32) for end in (0, 1)]
+        else:
+            beside = [corner_in[4 * (s - 1) + 2 * end + side] for end in (0, 1)]
+        term = dot(spread(None, None, s, y, beside), weight[8 - 3 * s - 2 * side])
+        part[side] = term if s == 0 else part[side] + term
+
     def add_part(s):
-        sums = []
-        for side, y in ((0, 0), (1, tall - 1)):
-            if s == 0:
-                beside = [col_in[0, end, y : y + 1, :].astype(F32) for end in (0, 1)]
-            else:
-                beside = [corner_in[4 * (s - 1) + 2 * end + side] for end in (0, 1)]
-            sums.append(dot(spread(None, None, s, y, beside), weight[8 - 3 * s - 2 * side]))
-        above, below = sums
-        if s == 0:
-            part[0] = above
-            part[1] = below
-        else:
-            part[0] += above
-            part[1] += below
+        add_side(s, 0)
+        add_side(s, 1)
+
+    def finish(s):
+        add_side(s, 1)
+        part_out[1] = part[1].astype(BF16)
+        pl.when(told > 0)(functools.partial(pl.semaphore_wait, far_sem, told))
+        start(part_copy, 1)
+        add_side(s, 0)
+        part_out[0] = part[0].astype(BF16)
+        start(part_copy, 0)
 
     def add_tile(s):
         for y in range(tall):
@@ -268,16 +276,21 @@
         @pl.when(t >= s)
         def _(s=s):
             took_sides(broad, 2, edge_recv.at[s - 1])
-            add_part(s)
-
-    part_out[...] = part[...].astype(BF16)
-    greeted = jnp.logical_and(odd, above)
-    up = part_copy(0)[0]
-    pl.when(greeted)(up.start)
-    told = jnp.where(odd, beyond.astype(jnp.int32) + jnp.logical_not(above).astype(jnp.int32), 1)
-    pl.when(told > 0)(functools.partial(pl.semaphore_wait, far_sem, told))
-    pl.when(jnp.logical_and(inside(0, -1, 0), jnp.logical_not(greeted)))(up.start)
-    start(part_copy, 1)
+            if s == 1:
+                pl.when(t == 1)(functools.partial(finish, 1))
+                pl.when(t > 1)(functools.partial(add_part, 1))
+            else:
+                finish(s)
+
+    @pl.when(t == 0)
+    def _():
+        part_out[...] = part[...].astype(BF16)
+        greeted = jnp.logical_and(odd, above)
+        up = part_copy(0)[0]
+        pl.when(greeted)(up.start)
+        pl.when(told > 0)(functools.partial(pl.semaphore_wait, far_sem, told))
+        pl.when(jnp.logical_and(inside(0, -1, 0), jnp.logical_not(greeted)))(up.start)
+        start(part_copy, 1)
 
     add_tile(0)
     for s in (1, 2):

time: 15.7 us -> 15.9 us (1.013)
    pallas_call x1, Pallas kernels: 15 us -> 15.1 us  [body(): pl.pallas_call(functools.partial(block_kernel, tall, broad, chans, frame_...]
where the time goes in v6:
time: 15.9 us; the launch traced here: 15.8 us
  Pallas kernels  15.1 us (95%)
  local copies, waits for them, and re-layouts  0.64 us (4%)
    pallas_call x1, Pallas kernels, body(): pl.pallas_call(functools.partial(block_kernel, tall, broad, chans, frame_...  15.1 us
    unnamed x1, local copies, waits for them, and re-layouts  0.64 us

profile of v6, /device:TPU:244, one launch (start us, length us, event | category | flops | bytes accessed | tf_op | source)
XLA Modules:
  0.0 15.8 jit_solution(205539102099656325)
XLA Ops:
  0.0 15.1 %causal_conv.1 = bf16[128,384]{1,0:T(8,128)(2,1)S(1)} custom-call(bf16[128,384]{1,0:T(8,128)(2,1)} %bitcast.5, f32[384]{0:T(512)} %gain_hbm.1, bf16[9,1152,384]{2,1,0:T(8,128)(2,1)} %bitcast.4, f32[384]{0:T(512)} %bias_hbm.1), custom_call_target="tpu_custom_call" | custom-call | tf_op jit(solution)/shard_map/causal_conv/pallas_call | solution.py:334
  15.2 0.6 %copy.6 = bf16[1,1,8,16,384]{4,3,2,1,0:T(8,128)(2,1)} copy(bf16[1,1,8,16,384]{4,3,2,1,0:T(8,128)(2,1)S(1)} %bitcast.3) | data formatting | bytes 196608
